TPU v7x, 256 devices: a whole 4x4x8 slice. The times are simulated.
256 devices in a mesh: field: 8 (over y, x_lo), azim: 32 (over z, x_hi, core).
Axes of the slice: x: 4 (x_hi: 2, x_lo: 2; x = x_hi * 2 + x_lo), y: 4, z: 8, core: 2. Of those that a mesh axis runs over, the one named last changes fastest.
Arguments:
- scalars: float32 [64, 10, 512, 1024], P('field', None, 'azim'), may hold values from -5 to 5
- wiener: float32 [64, 512, 1024], P('field', 'azim'), may hold values from -1.2 to 1.2
- velocity: float32 [512, 1024], P('azim', 'field'), may hold values from 0.5 to 2
- diffusivity: float32 [512, 1024], P('azim', 'field'), may hold values from 0.1 to 0.8
- mix_rate: float32 [512, 1024], P('azim', 'field'), may hold values from 0.5 to 4
- reaction_rate: float32 [10], replicated, may hold values from 0.2 to 1.5
- equilibrium: float32 [10], replicated, may hold values from -3 to 3
Outputs:
- advanced: float32 [64, 10, 512, 1024], P('field', None, 'azim')
- density: float32 [512, 1024], P('azim', 'field')
All inputs are finite; a program needn't handle non-finite values.
Results may differ from a plain program's by a relative error of at most 0.00002.
Values sent between devices are 32-bit elements; how exact they have to be, the bound alone decides.
A program may use at most 128 MiB of HBM per device.

v0:
```python
import jax
import jax.numpy as jnp
from jax import lax
from jax.sharding import PartitionSpec as P

NF = 64


step_size = 0.2


def sent_to_all(array, axis):
    count = lax.axis_size(axis)
    return lax.all_to_all(
        jnp.broadcast_to(array[None], (count, *array.shape)), axis, 0, 0, tiled=True
    )


def over_copies(array, axis):
    everything = sent_to_all(array, axis)
    return jnp.sum(everything, axis=0)


def with_halo(block, sides, width):
    for axis, dim in sides:
        count = lax.axis_size(axis)
        forward = [(i, i + 1) for i in range(count - 1)]
        forward.append((count - 1, 0))
        backward = [(target, source) for source, target in forward]
        low = lax.ppermute(
            lax.slice_in_dim(block, block.shape[dim] - width, None, axis=dim), axis, forward
        )
        high = lax.ppermute(lax.slice_in_dim(block, 0, width, axis=dim), axis, backward)
        block = jnp.concatenate([low, block, high], axis=dim)
    return block


def side_by_side(arrays, axis, dim, along):
    ends, at = ([], 0)
    for a in arrays[:-1]:
        at += a.shape[along]
        ends.append(at)
    both = jnp.concatenate(arrays, axis=along)
    return tuple(jnp.split(lax.all_gather(both, axis, axis=dim, tiled=True), ends, axis=along))


def cut_along(array, dim, count):
    shape = array.shape
    blocks = array.reshape(*shape[:dim], count, shape[dim] // count, *shape[dim + 1 :])
    return jnp.moveaxis(blocks, dim, 0)


def sum_at_owner(array, axis, dim):
    count = lax.axis_size(axis)
    blocks = lax.all_to_all(cut_along(array, dim, count), axis, 0, 0, tiled=True)
    return jnp.sum(blocks, axis=0)


def advance(
    middle,
    upper_row,
    lower_row,
    velocity,
    diffusivity,
    mix_rate,
    wiener,
    average,
    reaction_rate,
    equilibrium,
):
    gradient = 0.5 * (upper_row - lower_row)
    laplacian = upper_row - 2.0 * middle + lower_row
    heating = 1.0 + 0.5 * middle[:, 0] * middle[:, 0]
    burning = jnp.exp(1.0 - 1.0 / heating)
    source = (
        reaction_rate[None, :, None, None]
        * burning[:, None]
        * (equilibrium[None, :, None, None] - middle)
    )
    tendency = (
        -velocity * gradient
        + diffusivity * laplacian
        - 0.5 * mix_rate * (middle - average)
        + source
    )
    return middle + step_size * tendency + jnp.sqrt(2.0 * diffusivity) * gradient * wiener[:, None]


def field_average(local_sum):
    return over_copies(local_sum, "field") / NF


def rim_segment(state, gas_state, wiener, reaction_rate, equilibrium):
    padded = with_halo(state, (("azim", 2),), 1)
    average = field_average(jnp.sum(state, axis=0))
    return advance(
        state,
        padded[:, :, 2:],
        padded[:, :, :-2],
        gas_state[0],
        gas_state[1],
        gas_state[2],
        wiener,
        average,
        reaction_rate,
        equilibrium,
    )


def shards(scalars, wiener, velocity, diffusivity, mix_rate, reaction_rate, equilibrium):
    gas_state = side_by_side((velocity, diffusivity, mix_rate), "field", 1, 0)
    segment_one = rim_segment(scalars, gas_state, wiener, reaction_rate, equilibrium)
    segment_two = rim_segment(segment_one, gas_state, wiener, reaction_rate, equilibrium)
    advanced = 0.5 * scalars + 0.5 * segment_two
    heating = 1.0 + 0.5 * advanced[:, 0] * advanced[:, 0]
    totals = sum_at_owner(jnp.sum(heating, axis=0), "field", 1)
    density = 1.0 / (totals / NF)
    return (advanced, density)


def solution(mesh):
    return jax.shard_map(
        shards,
        mesh=mesh,
        in_specs=(
            P("field", None, "azim", None),
            P("field", "azim", None),
            P("azim", "field"),
            P("azim", "field"),
            P("azim", "field"),
            P(),
            P(),
        ),
        out_specs=(P("field", None, "azim", None), P("azim", "field")),
        check_vma=False,
    )
```

profile of v0, /device:TPU:2, one launch (start us, length us, event | category | flops | bytes accessed | tf_op | source)
XLA Modules:
  0.0 217.1 jit_solution(10133889651856172083)
XLA Ops:
  0.6 3.1 %reduce_sum.54 = f32[10,16,1024]{2,1,0:T(8,128)S(1)} reduce(f32[8,10,16,1024]{3,2,1,0:T(8,128)} %param.7, f32[]{:T(128)} %constant.8.clone.1), dimensions={0}, to_apply=%region_0.0 | reduce | flops 1146880 | bytes 5898244 | tf_op jit(solution)/shard_map/reduce_sum | solution.py:95
  3.7 3.0 %broadcast_in_dim.4 = f32[8,10,16,1024]{3,2,1,0:T(8,128)} broadcast(f32[10,16,1024]{2,1,0:T(8,128)S(1)} %reduce_sum.54), dimensions={1,2,3} | broadcast | bytes 5898240 | tf_op jit(solution)/shard_map/broadcast_in_dim | solution.py:15
  6.7 6.8 %all-to-all-start = ((f32[8,10,16,1024]{3,2,1,0:T(8,128)}), f32[8,10,16,1024]{3,2,1,0:T(8,128)}, u32[]{:S(2)}, u32[]{:S(2)}) async-start(f32[8,10,16,1024]{3,2,1,0:T(8,128)} %broadcast_in_dim.4), calls=%async_computation | async-start | bytes 10485760 | tf_op jit(solution)/shard_map/all_to_all | solution.py:14
  13.5 5.8 %copy.44 = f32[8,10,16,1024]{3,0,2,1:T(8,128)S(1)} copy(f32[8,10,16,1024]{3,2,1,0:T(8,128)} %param.7) | data formatting | bytes 10485760 | tf_op args[0]
  19.4 5.5 %collective-permute-start = (f32[8,10,1,1024]{3,0,2,1:T(8,128)S(1)}, f32[8,10,1,1024]{3,0,2,1:T(8,128)S(1)}, u32[]{:S(2)}, u32[]{:S(2)}) collective-permute-start(f32[8,10,1,1024]{3,0,2,1:T(8,128)S(1)} %get-tuple-element.12), channel_id=1, source_target_pairs={{1,0},{2,1},{3,2},{4,3},{5,4},{6,5},{7,6},{8,7},{9,8},{10,9},{11,1... | collective-permute-start | bytes 983048 | tf_op jit(solution)/shard_map/ppermute | solution.py:33
  24.9 73.3 %all_gather.3 = f32[48,1024]{1,0:T(8,128)S(1)} all-gather(f32[48,128]{1,0:T(8,128)S(1)} %pad_maximum_fusion.4), channel_id=1, replica_groups=mesh['field'=8,'azim'=32] {'field'}, dimensions={1}, use_global_device_ids=true | all-gather | bytes 221184 | tf_op jit(solution)/shard_map/all_gather | solution.py:44
  98.2 0.1 fusion.4
  98.4 0.3 copy.43
  98.7 3.1 %reduce_sum.55 = f32[10,16,1024]{2,1,0:T(8,128)S(1)} reduce(f32[8,10,16,1024]{3,2,1,0:T(8,128)} %all-to-all-done, f32[]{:T(128)} %constant.8.clone.1), dimensions={0}, to_apply=%region_1.0 | reduce | flops 1146880 | bytes 5898244 | tf_op jit(solution)/shard_map/reduce_sum | solution.py:21
  101.9 9.5 %fusion.13 = (f32[10,16,1024]{2,1,0:T(8,128)S(1)}, f32[8,10,16,1024]{3,0,2,1:T(8,128)}) fusion(f32[8,16,1024]{2,0,1:T(8,128)S(1)} %copy.43, f32[16,1024]{1,0:T(8,128)S(1)} %get-tuple-element.15, f32[8,10,16,1024]{3,0,2,1:T(8,128)} %copy-done, f32[10]{0:T(128)S(1)} %copy-done.6, f32[8,16,1024]{2,0,1:T(8,128)S(1)} %fusion.4, f32[10]{0:T(128)S(1)} %copy-done.7, ...), kind=kLoop, calls=%fused_computation.30 | loop fusion | flops 28672000 | bytes 13762640 | tf_op jit(solution)/shard_map/reduce_sum | solution.py:95
  111.4 3.0 %broadcast_in_dim.5 = f32[8,10,16,1024]{3,2,1,0:T(8,128)} broadcast(f32[10,16,1024]{2,1,0:T(8,128)S(1)} %get-tuple-element.8), dimensions={1,2,3} | broadcast | bytes 5898240 | tf_op jit(solution)/shard_map/broadcast_in_dim | solution.py:15
  114.4 8.0 %all-to-all-start.1 = ((f32[8,10,16,1024]{3,2,1,0:T(8,128)}), f32[8,10,16,1024]{3,2,1,0:T(8,128)}, u32[]{:S(2)}, u32[]{:S(2)}) async-start(f32[8,10,16,1024]{3,2,1,0:T(8,128)} %broadcast_in_dim.5), calls=%async_computation.1 | async-start | bytes 10485760 | tf_op jit(solution)/shard_map/all_to_all | solution.py:14
  122.4 1.1 fusion.14
  123.6 5.3 %collective-permute-start.2 = (f32[8,10,1,1024]{3,0,2,1:T(8,128)S(1)}, f32[8,10,1,1024]{3,0,2,1:T(8,128)S(1)}, u32[]{:S(2)}, u32[]{:S(2)}) collective-permute-start(f32[8,10,1,1024]{3,0,2,1:T(8,128)S(1)} %get-tuple-element.11), channel_id=1, source_target_pairs={{1,0},{2,1},{3,2},{4,3},{5,4},{6,5},{7,6},{8,7},{9,8},{10,9},{11,1... | collective-permute-start | bytes 983048 | tf_op jit(solution)/shard_map/ppermute | solution.py:33
  129.0 1.2 fusion.9
  130.2 53.2 %all-to-all-done.1 = f32[8,10,16,1024]{3,2,1,0:T(8,128)} async-done(((f32[8,10,16,1024]{3,2,1,0:T(8,128)}), f32[8,10,16,1024]{3,2,1,0:T(8,128)}, u32[]{:S(2)}, u32[]{:S(2)}) %all-to-all-start.1) | async-done | bytes 5242912 | tf_op jit(solution)/shard_map/all_to_all | solution.py:14
  183.4 3.1 %reduce_sum.57 = f32[10,16,1024]{2,1,0:T(8,128)S(1)} reduce(f32[8,10,16,1024]{3,2,1,0:T(8,128)} %all-to-all-done.1, f32[]{:T(128)} %constant.8.clone.1), dimensions={0}, to_apply=%region_3.0 | reduce | flops 1146880 | bytes 5898244 | tf_op jit(solution)/shard_map/reduce_sum | solution.py:21
  186.5 12.0 %add_multiply_fusion = f32[8,10,16,1024]{3,0,2,1:T(8,128)S(1)} fusion(f32[8,10,16,1024]{3,0,2,1:T(8,128)} %get-tuple-element.9, f32[8,10,1,1024]{3,0,2,1:T(8,128)S(1)} %collective-permute-done.2, f32[8,10,1,1024]{3,0,2,1:T(8,128)S(1)} %collective-permute-done.3, f32[8,16,1024]{2,0,1:T(8,128)S(1)} %fusion.9, f32[10,16,1024]{2,1,0:T(8,128)S(1)} %broadcast_multiply_fusion, ...), kind=kLoop, calls=%fused_computation.4 | loop fusion | flops 30146560 | bytes 18350160 | tf_op jit(solution)/shard_map/add | solution.py:114
  198.6 2.3 %copy-done.1 = f32[8,10,16,1024]{3,0,2,1:T(8,128)} copy-done((f32[8,10,16,1024]{3,0,2,1:T(8,128)}, f32[8,10,16,1024]{3,0,2,1:T(8,128)S(1)}, u32[]{:S(2)}) %copy-start.1) | copy-done | bytes 5242904
  200.9 0.2 fusion.11
  201.1 0.6 copy.45
  201.7 6.8 %all-to-all-start.2 = ((f32[8,16,128]{2,1,0:T(8,128)}), f32[8,16,128]{2,1,0:T(8,128)S(1)}, u32[]{:S(2)}, u32[]{:S(2)}) async-start(f32[8,16,128]{2,1,0:T(8,128)} %copy.45), calls=%async_computation.2 | async-start | bytes 131072 | tf_op jit(solution)/shard_map/all_to_all | solution.py:55
  208.6 7.9 %copy.46 = f32[8,10,16,1024]{3,2,1,0:T(8,128)} copy(f32[8,10,16,1024]{3,0,2,1:T(8,128)} %copy-done.1) | data formatting | bytes 10485760
  216.5 0.6 multiply_divide_fusion
  (30 shorter events, 0.3 us)
Async XLA Ops:
  6.7 92.0 %all-to-all-start = ((f32[8,10,16,1024]{3,2,1,0:T(8,128)}), f32[8,10,16,1024]{3,2,1,0:T(8,128)}, u32[]{:S(2)}, u32[]{:S(2)}) async-start(f32[8,10,16,1024]{3,2,1,0:T(8,128)} %broadcast_in_dim.4), calls=%async_computation | async-start | bytes 10485760 | tf_op jit(solution)/shard_map/all_to_all | solution.py:14
  13.5 11.4 %copy-start.3 = (f32[16,128]{1,0:T(8,128)S(1)}, f32[16,128]{1,0:T(8,128)}, u32[]{:S(2)}) copy-start(f32[16,128]{1,0:T(8,128)} %param.11) | copy-start | bytes 24580
  13.5 11.4 %copy-start.4 = (f32[16,128]{1,0:T(8,128)S(1)}, f32[16,128]{1,0:T(8,128)}, u32[]{:S(2)}) copy-start(f32[16,128]{1,0:T(8,128)} %param.10) | copy-start | bytes 24580
  13.5 11.4 %copy-start.5 = (f32[16,128]{1,0:T(8,128)S(1)}, f32[16,128]{1,0:T(8,128)}, u32[]{:S(2)}) copy-start(f32[16,128]{1,0:T(8,128)} %param.9) | copy-start | bytes 24580
  13.5 84.9 %copy-start.2 = (f32[8,16,1024]{2,1,0:T(8,128)S(1)}, f32[8,16,1024]{2,1,0:T(8,128)}, u32[]{:S(2)}) copy-start(f32[8,16,1024]{2,1,0:T(8,128)} %param.8) | copy-start | bytes 1572868
  19.3 78.9 %copy-start = (f32[8,10,16,1024]{3,0,2,1:T(8,128)}, f32[8,10,16,1024]{3,0,2,1:T(8,128)S(1)}, u32[]{:S(2)}) copy-start(f32[8,10,16,1024]{3,0,2,1:T(8,128)S(1)} %copy.44) | copy-start | bytes 15728644
  19.4 82.5 %copy-start.6 = (f32[10]{0:T(128)S(1)}, f32[10]{0:T(128)}, u32[]{:S(2)}) copy-start(f32[10]{0:T(128)} %param.13) | copy-start | bytes 124
  19.4 82.5 %copy-start.7 = (f32[10]{0:T(128)S(1)}, f32[10]{0:T(128)}, u32[]{:S(2)}) copy-start(f32[10]{0:T(128)} %param.12) | copy-start | bytes 124
  19.4 82.5 %collective-permute-start = (f32[8,10,1,1024]{3,0,2,1:T(8,128)S(1)}, f32[8,10,1,1024]{3,0,2,1:T(8,128)S(1)}, u32[]{:S(2)}, u32[]{:S(2)}) collective-permute-start(f32[8,10,1,1024]{3,0,2,1:T(8,128)S(1)} %get-tuple-element.12), channel_id=1, source_target_pairs={{1,0},{2,1},{3,2},{4,3},{5,4},{6,5},{7,6},{8,7},{9,8},{10,9},{11,1... | collective-permute-start | bytes 983048 | tf_op jit(solution)/shard_map/ppermute | solution.py:33
  24.9 77.0 %collective-permute-start.1 = (f32[8,10,1,1024]{3,0,2,1:T(8,128)S(1)}, f32[8,10,1,1024]{3,0,2,1:T(8,128)S(1)}, u32[]{:S(2)}, u32[]{:S(2)}) collective-permute-start(f32[8,10,1,1024]{3,0,2,1:T(8,128)S(1)} %get-tuple-element.13), channel_id=1, source_target_pairs={{0,1},{1,2},{2,3},{3,4},{4,5},{5,6},{6,7},{7,8},{8,9},{9,10},{10,1... | collective-permute-start | bytes 983048 | tf_op jit(solution)/shard_map/ppermute | solution.py:30
  114.4 68.9 %all-to-all-start.1 = ((f32[8,10,16,1024]{3,2,1,0:T(8,128)}), f32[8,10,16,1024]{3,2,1,0:T(8,128)}, u32[]{:S(2)}, u32[]{:S(2)}) async-start(f32[8,10,16,1024]{3,2,1,0:T(8,128)} %broadcast_in_dim.5), calls=%async_computation.1 | async-start | bytes 10485760 | tf_op jit(solution)/shard_map/all_to_all | solution.py:14
  123.5 63.0 %collective-permute-start.3 = (f32[8,10,1,1024]{3,0,2,1:T(8,128)S(1)}, f32[8,10,1,1024]{3,0,2,1:T(8,128)S(1)}, u32[]{:S(2)}, u32[]{:S(2)}) collective-permute-start(f32[8,10,1,1024]{3,0,2,1:T(8,128)S(1)} %get-tuple-element.10), channel_id=1, source_target_pairs={{0,1},{1,2},{2,3},{3,4},{4,5},{5,6},{6,7},{7,8},{8,9},{9,10},{10,1... | collective-permute-start | bytes 983048 | tf_op jit(solution)/shard_map/ppermute | solution.py:30
  123.6 62.9 %collective-permute-start.2 = (f32[8,10,1,1024]{3,0,2,1:T(8,128)S(1)}, f32[8,10,1,1024]{3,0,2,1:T(8,128)S(1)}, u32[]{:S(2)}, u32[]{:S(2)}) collective-permute-start(f32[8,10,1,1024]{3,0,2,1:T(8,128)S(1)} %get-tuple-element.11), channel_id=1, source_target_pairs={{1,0},{2,1},{3,2},{4,3},{5,4},{6,5},{7,6},{8,7},{9,8},{10,9},{11,1... | collective-permute-start | bytes 983048 | tf_op jit(solution)/shard_map/ppermute | solution.py:33
  198.6 2.3 %copy-start.1 = (f32[8,10,16,1024]{3,0,2,1:T(8,128)}, f32[8,10,16,1024]{3,0,2,1:T(8,128)S(1)}, u32[]{:S(2)}) copy-start(f32[8,10,16,1024]{3,0,2,1:T(8,128)S(1)} %add_multiply_fusion) | copy-start | bytes 15728644
  201.7 14.7 %all-to-all-start.2 = ((f32[8,16,128]{2,1,0:T(8,128)}), f32[8,16,128]{2,1,0:T(8,128)S(1)}, u32[]{:S(2)}, u32[]{:S(2)}) async-start(f32[8,16,128]{2,1,0:T(8,128)} %copy.45), calls=%async_computation.2 | async-start | bytes 131072 | tf_op jit(solution)/shard_map/all_to_all | solution.py:55
where the time goes:
time: 218 us; the launch traced here: 217 us
  blocking collectives  73.3 us (34%)
  waiting for transfers between devices  53.2 us (24%)
  other arithmetic  33 us (15%)
  starting transfers between devices  32.5 us (15%)
  local copies, waits for them, and re-layouts  24.1 us (11%)
    all_gather x1, blocking collectives, side_by_side(): lax.all_gather(both, axis, axis=dim, tiled=True)  73.3 us
    all_to_all x2, waiting for transfers between devices, sent_to_all(): lax.all_to_all(jnp.broadcast_to(array[None], (count, *array.shape)), axis...  53.2 us
    unnamed x20, local copies, waits for them, and re-layouts  16.3 us
    all_to_all x2, starting transfers between devices, sent_to_all(): lax.all_to_all(jnp.broadcast_to(array[None], (count, *array.shape)), axis...  14.8 us
    reduce_sum x2, other arithmetic, rim_segment(): average = field_average(jnp.sum(state, axis=0))  12.6 us
    add x1, other arithmetic, shards(): advanced = 0.5 * scalars + 0.5 * segment_two  12 us
    ppermute x2, starting transfers between devices, with_halo(): lax.ppermute(lax.slice_in_dim(block, 0, width, axis=dim), axis, backward)  10.8 us
    all_to_all x1, starting transfers between devices, sum_at_owner(): lax.all_to_all(cut_along(array, dim, count), axis, 0, 0, tiled=True)  6.84 us
  transfers between devices with their start and end apart: 7, of which 1 were waited for; matrix products, arithmetic and copies ran while one was open for 10% of the time, Pallas kernels for 0%

commit v1 on v0

v1 whole, which is shorter than its diff:
```python
import functools

import jax
import jax.numpy as jnp
from jax import lax
from jax.experimental import pallas as pl
from jax.experimental.pallas import tpu as pltpu
from jax.sharding import PartitionSpec as P

MESH = pl.DeviceIdType.MESH
NF = 64
DT = 0.2
FL = 8
NS = 10
ROWS = 16
CELLS = 1024
QUARTER = 256
CHUNK = 128
HALF = NS // 2


def kernel(
    n_az,
    q_in, w_in, vel_in, dif_in, mix_in, rate, equil,
    adv_out, den_out,
    q, u, w, gas, gas_own, h1, h2, sums, got1, got2, got3, total, e2, heat, heat_got,
    load_sem, out_sem, gas_s, gas_r, h1_s, h1_r, h2_s, h2_r, red_s, red_r, den_s, den_r,
):
    f = lax.axis_index("field")
    a = lax.axis_index("azim")
    y, xl = f // 2, f % 2
    yp, yo, ym = (y + 1) % 4, (y + 2) % 4, (y + 3) % 4
    dev_p, dev_m, dev_x = (yp * 2 + xl, a), (ym * 2 + xl, a), (y * 2 + 1 - xl, a)
    dev_up, dev_dn = (f, (a + 1) % n_az), (f, (a + n_az - 1) % n_az)

    def peer(k):
        return ((f + k) % 8, a)

    def chunk(i):
        return pl.ds(pl.multiple_of(i * CHUNK, CHUNK), CHUNK)

    def quarter(i):
        return pl.ds(pl.multiple_of(i * QUARTER, QUARTER), QUARTER)

    def remote(src, dst, send, recv, device):
        return pltpu.make_async_remote_copy(
            src_ref=src, dst_ref=dst, send_sem=send, recv_sem=recv,
            device_id=device, device_id_type=MESH,
        )

    loads = [pltpu.make_async_copy(q_in.at[i], q.at[i], load_sem.at[i]) for i in range(FL)]
    gas_loads = [
        pltpu.make_async_copy(r, gas_own.at[i], load_sem.at[FL + 1 + i])
        for i, r in enumerate((vel_in, dif_in, mix_in))
    ]
    w_load = pltpu.make_async_copy(w_in, w, load_sem.at[FL])
    for c in gas_loads + loads + [w_load]:
        c.start()

    barrier = pltpu.get_barrier_semaphore()
    greeted = [peer(k) for k in range(1, 8)] + [dev_up, dev_dn]
    for d in greeted:
        pl.semaphore_signal(barrier, inc=1, device_id=d, device_id_type=MESH)
    pl.semaphore_wait(barrier, len(greeted))

    halo1 = [
        remote(q_in.at[:, :, pl.ds(ROWS - 1, 1), :], h1.at[0], h1_s.at[0], h1_r.at[0], dev_up),
        remote(q_in.at[:, :, pl.ds(0, 1), :], h1.at[1], h1_s.at[1], h1_r.at[1], dev_dn),
    ]
    for c in gas_loads:
        c.wait()
    gas_sends = [
        remote(gas_own, gas.at[:, :, chunk(f)], gas_s.at[k], gas_r.at[k], peer(k + 1))
        for k in range(7)
    ]
    for c in gas_sends:
        c.start()
    for c in halo1:
        c.start()
    gas[:, :, chunk(f)] = gas_own[...]
    for c in loads:
        c.wait()

    def red(n, i, src, dst, device):
        return remote(src, dst, red_s.at[n, i], red_r.at[n, i], device)

    lo, hi = pl.ds(0, HALF), pl.ds(HALF, HALF)

    def step1(n):
        return [
            red(n, 0, sums.at[n, lo, :, quarter(yo)], got1.at[n, 0], dev_p),
            red(n, 1, sums.at[n, hi, :, quarter(yo)], got1.at[n, 1], dev_m),
        ]

    def step2a(n):
        return [
            red(n, 2, sums.at[n, hi, :, quarter(yp)], got2.at[n, 0, hi], dev_p),
            red(n, 3, sums.at[n, lo, :, quarter(ym)], got2.at[n, 1, lo], dev_m),
        ]

    def step2b(n):
        return [
            red(n, 4, sums.at[n, lo, :, quarter(yp)], got2.at[n, 0, lo], dev_p),
            red(n, 5, sums.at[n, hi, :, quarter(ym)], got2.at[n, 1, hi], dev_m),
        ]

    def step3(n):
        return red(n, 6, sums.at[n, :, :, chunk(y * 2 + 1 - xl)], got3.at[n], dev_x)

    def gather_own(n):
        piece = total.at[n, :, :, chunk(f)]
        return [red(n, 7, piece, piece, dev_x), red(n, 8, piece, piece, dev_p), red(n, 9, piece, piece, dev_m)]

    def gather_x(n):
        piece = total.at[n, :, :, chunk(y * 2 + 1 - xl)]
        return [red(n, 10, piece, piece, dev_p), red(n, 11, piece, piece, dev_m)]

    def pass_on(n, which):
        side = xl if which == 0 else 1 - xl
        from_m = total.at[n, lo, :, chunk(ym * 2 + side)]
        from_p = total.at[n, hi, :, chunk(yp * 2 + side)]
        return [
            red(n, 12 + 2 * which, from_m, from_m, dev_p),
            red(n, 13 + 2 * which, from_p, from_p, dev_m),
        ]

    def start(copies):
        for c in copies:
            c.start()

    def arrive(copies):
        for c in copies:
            c.wait_recv()

    def after1(n):
        arrive(step1(n))

        def body(s, _):
            sums[n, s, :, quarter(yp)] += got1[n, 0, s]
            sums[n, HALF + s, :, quarter(ym)] += got1[n, 1, s]
            return 0

        lax.fori_loop(0, HALF, body, 0)
        start(step2b(n))

    def after2(n):
        arrive(step2a(n) + step2b(n))

        def body(s, _):
            sums[n, s, :, quarter(y)] += got2[n, 0, s] + got2[n, 1, s]
            return 0

        lax.fori_loop(0, NS, body, 0)
        step3(n).start()

    def after3(n):
        step3(n).wait_recv()

        def body(s, _):
            total[n, s, :, chunk(f)] = sums[n, s, :, chunk(f)] + got3[n, s]
            return 0

        lax.fori_loop(0, NS, body, 0)
        start(gather_own(n))

    def after_x(n):
        gather_own(n)[0].wait_recv()
        start(gather_x(n))

    def after_own(n):
        arrive(gather_own(n)[1:])
        start(pass_on(n, 0))

    def after_partner(n):
        arrive(gather_x(n))
        start(pass_on(n, 1))

    def after_all(n):
        arrive(pass_on(n, 0) + pass_on(n, 1))

    def sum_q(k):
        def body(s, _):
            acc = q[0, s, :, quarter(k)]
            for i in range(1, FL):
                acc = acc + q[i, s, :, quarter(k)]
            sums[0, s, :, quarter(k)] = acc
            return 0

        lax.fori_loop(0, NS, body, 0)

    sum_q(yo)
    start(step1(0))
    sum_q(yp)
    step2a(0)[0].start()
    sum_q(ym)
    step2a(0)[1].start()
    sum_q(y)
    after1(0)

    row = lax.broadcasted_iota(jnp.int32, (8, CHUNK), 0)
    first, last = row == 0, row == 7
    tiles = (pl.ds(0, 8), pl.ds(8, 8))

    def neighbours(lower, upper, below, above):
        lower_up, upper_up = pltpu.roll(lower, 7, 0), pltpu.roll(upper, 7, 0)
        lower_dn, upper_dn = pltpu.roll(lower, 1, 0), pltpu.roll(upper, 1, 0)
        up = (jnp.where(last, upper_up, lower_up), jnp.where(last, above, upper_up))
        dn = (jnp.where(first, below, lower_dn), jnp.where(first, lower_dn, upper_dn))
        return up, dn

    def coefficients(cols, t):
        vel, dif, mix = gas[0, tiles[t], cols], gas[1, tiles[t], cols], gas[2, tiles[t], cols]
        keep = 1.0 - (2.0 * DT) * dif - (0.5 * DT) * mix
        return keep, DT * dif, (-0.5 * DT) * vel, 0.5 * jnp.sqrt(2.0 * dif)

    def burn(x):
        heating = 1.0 + 0.5 * x * x
        return DT * jnp.exp(1.0 - 1.0 / heating)

    def explicit(k):
        def column(j, _):
            cols = chunk(k * 2 + j)
            co = [coefficients(cols, t) for t in range(2)]

            def field(i, acc):
                grad_c = [co[t][2] + co[t][3] * w[i, tiles[t], cols] for t in range(2)]
                b = [burn(q[i, 0, tiles[t], cols]) for t in range(2)]
                out = []
                for s in range(NS):
                    x = [q[i, s, tiles[t], cols] for t in range(2)]
                    below = jnp.broadcast_to(h1[0, i, s, :, cols], (8, CHUNK))
                    above = jnp.broadcast_to(h1[1, i, s, :, cols], (8, CHUNK))
                    up, dn = neighbours(x[0], x[1], below, above)
                    for t in range(2):
                        v = (
                            x[t] * co[t][0]
                            + (up[t] - dn[t]) * grad_c[t]
                            + (up[t] + dn[t]) * co[t][1]
                            + (rate[s] * b[t]) * (equil[s] - x[t])
                        )
                        u[i, s, tiles[t], cols] = v
                        out.append(acc[2 * s + t] + v)
                return tuple(out)

            acc = lax.fori_loop(0, FL, field, (jnp.zeros((8, CHUNK), jnp.float32),) * (2 * NS))
            for s in range(NS):
                for t in range(2):
                    sums[1, s, tiles[t], cols] = acc[2 * s + t]
            return 0

        lax.fori_loop(0, 2, column, 0)

    after2(0)
    arrive(gas_sends)
    w_load.wait()
    arrive(halo1)
    explicit(yo)
    start(step1(1))
    after3(0)
    explicit(yp)
    step2a(1)[0].start()
    after_x(0)
    explicit(ym)
    step2a(1)[1].start()
    explicit(y)
    after1(1)
    after_own(0)
    after_partner(0)

    def halo2(k, i):
        cols = quarter(k)
        return [
            remote(u.at[:, :, pl.ds(ROWS - 1, 1), cols], h2.at[0, :, :, :, cols], h2_s.at[0, i], h2_r.at[0, i], dev_up),
            remote(u.at[:, :, pl.ds(0, 1), cols], h2.at[1, :, :, :, cols], h2_s.at[1, i], h2_r.at[1, i], dev_dn),
        ]

    def mixed(k, n):
        def body(s, _):
            cols = quarter(k)
            e = (0.5 * DT / NF) * gas[2, :, cols] * total[0, s, :, cols]
            for i in range(FL):
                u[i, s, :, cols] += e
            return 0

        lax.fori_loop(0, NS, body, 0)
        start(halo2(k, n))

    mixed(y, 0)
    after2(1)
    mixed(ym, 1)
    mixed(yp, 2)
    after3(1)
    after_all(0)
    mixed(yo, 3)
    after_x(1)

    def second(k, n):
        cols_q = quarter(k)

        def column(j, _):
            cols = chunk(k * 2 + j)
            co = [coefficients(cols, t) for t in range(2)]
            for s in range(NS):
                for t in range(2):
                    m = (0.5 * DT) * gas[2, tiles[t], cols]
                    first_mean = m * total[0, s, tiles[t], cols]
                    e2[s, tiles[t], :] = (0.5 / NF) * m * (total[1, s, tiles[t], cols] + first_mean)
            half = [tuple(0.5 * c for c in co[t]) for t in range(2)]

            def field(i, acc):
                grad_c = [half[t][2] + half[t][3] * w[i, tiles[t], cols] for t in range(2)]
                b = [0.5 * burn(u[i, 0, tiles[t], cols]) for t in range(2)]
                out = list(acc)
                for s in range(NS):
                    x = [u[i, s, tiles[t], cols] for t in range(2)]
                    below = jnp.broadcast_to(h2[0, i, s, :, cols], (8, CHUNK))
                    above = jnp.broadcast_to(h2[1, i, s, :, cols], (8, CHUNK))
                    up, dn = neighbours(x[0], x[1], below, above)
                    for t in range(2):
                        v = (
                            0.5 * q[i, s, tiles[t], cols]
                            + x[t] * half[t][0]
                            + (up[t] - dn[t]) * grad_c[t]
                            + (up[t] + dn[t]) * half[t][1]
                            + e2[s, tiles[t], :]
                            + (rate[s] * b[t]) * (equil[s] - x[t])
                        )
                        q[i, s, tiles[t], cols] = v
                        if s == 0:
                            out[t] = out[t] + (1.0 + 0.5 * v * v)
                return tuple(out)

            acc = lax.fori_loop(0, FL, field, (jnp.zeros((8, CHUNK), jnp.float32),) * 2)
            for t in range(2):
                heat[tiles[t], cols] = acc[t]
            return 0

        for c in halo2(k, n):
            c.wait_recv()
        lax.fori_loop(0, 2, column, 0)

    def write(k, n):
        cols = quarter(k)
        return pltpu.make_async_copy(q.at[:, :, :, cols], adv_out.at[:, :, :, cols], out_sem.at[n])

    def den(k, n):
        out = []
        for side in range(2):
            owner = k * 2 + (xl + side) % 2
            out.append(
                remote(heat.at[:, chunk(owner)], heat_got.at[n, side], den_s.at[n, side], den_r.at[n, side], (owner, a))
            )
        return out

    second(y, 0)
    den(y, 0)[1].start()
    write(y, 0).start()
    after_own(1)
    after_partner(1)
    second(ym, 1)
    start(den(ym, 1))
    write(ym, 1).start()
    second(yp, 2)
    start(den(yp, 2))
    write(yp, 2).start()
    after_all(1)
    second(yo, 3)
    start(den(yo, 3))
    write(yo, 3).start()

    heat_sum = heat[:, chunk(f)]
    den(y, 0)[1].wait_recv()
    heat_sum = heat_sum + heat_got[0, 1]
    for n, k in ((1, ym), (2, yp), (3, yo)):
        arrive(den(k, n))
        heat_sum = heat_sum + heat_got[n, 0] + heat_got[n, 1]
    den_out[...] = 1.0 / (heat_sum * (1.0 / NF))

    for c in gas_sends + halo1:
        c.wait_send()
    for n in range(2):
        copies = step1(n) + step2a(n) + step2b(n) + [step3(n)] + gather_own(n) + gather_x(n) + pass_on(n, 0) + pass_on(n, 1)
        for c in copies:
            c.wait_send()
    den(y, 0)[1].wait_send()
    for n, k in ((0, y), (1, ym), (2, yp), (3, yo)):
        for c in halo2(k, n):
            c.wait_send()
        if n:
            for c in den(k, n):
                c.wait_send()
        write(k, n).wait()


def solution(mesh):
    n_az = mesh.shape["azim"]

    def shards(scalars, wiener, velocity, diffusivity, mix_rate, reaction_rate, equilibrium):
        any_ = pl.BlockSpec(memory_space=pl.ANY)
        smem = pl.BlockSpec(memory_space=pltpu.SMEM)
        f32 = jnp.float32
        dma = pltpu.SemaphoreType.DMA
        return pl.pallas_call(
            functools.partial(kernel, n_az),
            out_shape=(
                jax.ShapeDtypeStruct((FL, NS, ROWS, CELLS), f32),
                jax.ShapeDtypeStruct((ROWS, CHUNK), f32),
            ),
            in_specs=[any_] * 5 + [smem] * 2,
            out_specs=(any_, pl.BlockSpec(memory_space=pltpu.VMEM)),
            scratch_shapes=[
                pltpu.VMEM((FL, NS, ROWS, CELLS), f32),
                pltpu.VMEM((FL, NS, ROWS, CELLS), f32),
                pltpu.VMEM((FL, ROWS, CELLS), f32),
                pltpu.VMEM((3, ROWS, CELLS), f32),
                pltpu.VMEM((3, ROWS, CHUNK), f32),
                pltpu.VMEM((2, FL, NS, 1, CELLS), f32),
                pltpu.VMEM((2, FL, NS, 1, CELLS), f32),
                pltpu.VMEM((2, NS, ROWS, CELLS), f32),
                pltpu.VMEM((2, 2, HALF, ROWS, QUARTER), f32),
                pltpu.VMEM((2, 2, NS, ROWS, QUARTER), f32),
                pltpu.VMEM((2, NS, ROWS, CHUNK), f32),
                pltpu.VMEM((2, NS, ROWS, CELLS), f32),
                pltpu.VMEM((NS, ROWS, CHUNK), f32),
                pltpu.VMEM((ROWS, CELLS), f32),
                pltpu.VMEM((4, 2, ROWS, CHUNK), f32),
                dma((FL + 4,)), dma((4,)),
                dma((7,)), dma((7,)),
                dma((2,)), dma((2,)),
                dma((2, 4)), dma((2, 4)),
                dma((2, 16)), dma((2, 16)),
                dma((4, 2)), dma((4, 2)),
            ],
            compiler_params=pltpu.CompilerParams(
                collective_id=0, has_side_effects=True, vmem_limit_bytes=48 << 20
            ),
            name="fields_step",
        )(scalars, wiener, velocity, diffusivity, mix_rate, reaction_rate, equilibrium)

    return jax.shard_map(
        shards,
        mesh=mesh,
        in_specs=(
            P("field", None, "azim", None),
            P("field", "azim", None),
            P("azim", "field"),
            P("azim", "field"),
            P("azim", "field"),
            P(),
            P(),
        ),
        out_specs=(P("field", None, "azim", None), P("azim", "field")),
        check_vma=False,
    )
```

time: 218 us -> 62.9 us (0.29)
  blocking collectives: 73.3 us -> 0 us
  Pallas kernels: 0 us -> 54 us
  waiting for transfers between devices: 53.2 us -> 0 us
  other arithmetic: 33 us -> 0 us
  starting transfers between devices: 32.5 us -> 0 us
  local copies, waits for them, and re-layouts: 24.1 us -> 7.39 us
    all_gather x1 -> x0, blocking collectives: 73.3 us -> none  [side_by_side(): lax.all_gather(both, axis, axis=dim, tiled=True)]
    pallas_call x0 -> x1, Pallas kernels: none -> 54 us  [shards(): pl.pallas_call(functools.partial(kernel, n_az), out_shape=(jax.ShapeDtype...]
    all_to_all x3 -> x0, waiting for transfers between devices: 53.2 us -> none  [the longest x2 53.2 us: sent_to_all(): lax.all_to_all(jnp.broadcast_to(array[None], (count, *array.shape)), axis...]
    all_to_all x3 -> x0, starting transfers between devices: 21.6 us -> none  [the longest x2 14.8 us: sent_to_all(): lax.all_to_all(jnp.broadcast_to(array[None], (count, *array.shape)), axis...]
    reduce_sum x6 -> x0, other arithmetic: 18.9 us -> none  [the longest x2 12.6 us: rim_segment(): average = field_average(jnp.sum(state, axis=0))]
    add x1 -> x0, other arithmetic: 12 us -> none  [shards(): advanced = 0.5 * scalars + 0.5 * segment_two]
    ppermute x4 -> x0, starting transfers between devices: 10.9 us -> none  [the longest x2 10.8 us: with_halo(): lax.ppermute(lax.slice_in_dim(block, 0, width, axis=dim), axis, backward)]
    unnamed x20 -> x14, local copies, waits for them, and re-layouts: 16.3 us -> 7.39 us
  transfers between devices with their start and end apart: 7 -> 0, of which waited for: 1 -> 0; matrix products, arithmetic and copies ran while one was open for 10% -> 0% of each run, Pallas kernels for 0% -> 0%
where the time goes in v1:
time: 62.9 us; the launch traced here: 62 us
  Pallas kernels  54 us (86%)
  local copies, waits for them, and re-layouts  7.39 us (12%)
  between operations  0.65 us (1%)
    pallas_call x1, Pallas kernels, shards(): pl.pallas_call(functools.partial(kernel, n_az), out_shape=(jax.ShapeDtype...  54 us
    unnamed x14, local copies, waits for them, and re-layouts  7.39 us

profile of v1, /device:TPU:2, one launch (start us, length us, event | category | flops | bytes accessed | tf_op | source)
XLA Modules:
  0.0 62.0 jit_solution(12957246874544143778)
XLA Ops:
  0.6 0.0 copy-start
  0.6 1.0 %copy-done = f32[8,16,1024]{2,1,0:T(8,128)S(1)} copy-done((f32[8,16,1024]{2,1,0:T(8,128)S(1)}, f32[8,16,1024]{2,1,0:T(8,128)}, u32[]{:S(2)}) %copy-start) | copy-done | bytes 524312
  1.7 0.0 copy-start.1
  1.7 0.7 %copy-done.1 = f32[16,128]{1,0:T(8,128)S(1)} copy-done((f32[16,128]{1,0:T(8,128)S(1)}, f32[16,128]{1,0:T(8,128)}, u32[]{:S(2)}) %copy-start.1) | copy-done | bytes 8216
  2.4 0.0 copy-start.2
  2.4 0.7 %copy-done.2 = f32[16,128]{1,0:T(8,128)S(1)} copy-done((f32[16,128]{1,0:T(8,128)S(1)}, f32[16,128]{1,0:T(8,128)}, u32[]{:S(2)}) %copy-start.2) | copy-done | bytes 8216
  3.1 0.0 copy-start.3
  3.1 0.7 %copy-done.3 = f32[16,128]{1,0:T(8,128)S(1)} copy-done((f32[16,128]{1,0:T(8,128)S(1)}, f32[16,128]{1,0:T(8,128)}, u32[]{:S(2)}) %copy-start.3) | copy-done | bytes 8216
  3.8 0.0 copy-start.4
  3.8 0.7 %copy-done.4 = f32[10]{0:T(128)S(1)} copy-done((f32[10]{0:T(128)S(1)}, f32[10]{0:T(128)}, u32[]{:S(2)}) %copy-start.4) | copy-done | bytes 64
  4.4 0.0 copy-start.5
  4.4 0.7 %copy-done.5 = f32[10]{0:T(128)S(1)} copy-done((f32[10]{0:T(128)S(1)}, f32[10]{0:T(128)}, u32[]{:S(2)}) %copy-start.5) | copy-done | bytes 64
  5.1 54.0 %fields_step.1 = (f32[8,10,16,1024]{3,2,1,0:T(8,128)S(1)}, f32[16,128]{1,0:T(8,128)S(1)}) custom-call(f32[8,10,16,1024]{3,2,1,0:T(8,128)} %q_in.1, f32[8,16,1024]{2,1,0:T(8,128)S(1)} %copy-done, f32[16,128]{1,0:T(8,128)S(1)} %copy-done.1, f32[16,128]{1,0:T(8,128)S(1)} %copy-done.2, f32[16,128]{1,0:T(8,128)S(1)} %copy-done.3, f32[10]{0:T(128)S(1)} %copy-done.4, ...), custom_call_target="tpu_custom_call" | custom-call | tf_op jit(solution)/shard_map/fields_step/pallas_call | solution.py:403
  59.1 2.4 %copy.11 = f32[8,10,16,1024]{3,2,1,0:T(8,128)} copy(f32[8,10,16,1024]{3,2,1,0:T(8,128)S(1)} %get-tuple-element.4) | data formatting | bytes 10485760
  61.4 0.6 copy.12
Async XLA Ops:
  0.6 1.0 %copy-start = (f32[8,16,1024]{2,1,0:T(8,128)S(1)}, f32[8,16,1024]{2,1,0:T(8,128)}, u32[]{:S(2)}) copy-start(f32[8,16,1024]{2,1,0:T(8,128)} %w_in.1) | copy-start | bytes 1572868
  1.7 0.7 %copy-start.1 = (f32[16,128]{1,0:T(8,128)S(1)}, f32[16,128]{1,0:T(8,128)}, u32[]{:S(2)}) copy-start(f32[16,128]{1,0:T(8,128)} %vel_in.1) | copy-start | bytes 24580
  2.4 0.7 %copy-start.2 = (f32[16,128]{1,0:T(8,128)S(1)}, f32[16,128]{1,0:T(8,128)}, u32[]{:S(2)}) copy-start(f32[16,128]{1,0:T(8,128)} %dif_in.1) | copy-start | bytes 24580
  3.1 0.7 %copy-start.3 = (f32[16,128]{1,0:T(8,128)S(1)}, f32[16,128]{1,0:T(8,128)}, u32[]{:S(2)}) copy-start(f32[16,128]{1,0:T(8,128)} %mix_in.1) | copy-start | bytes 24580
  3.8 0.7 %copy-start.4 = (f32[10]{0:T(128)S(1)}, f32[10]{0:T(128)}, u32[]{:S(2)}) copy-start(f32[10]{0:T(128)} %rate.1) | copy-start | bytes 124
  4.4 0.7 %copy-start.5 = (f32[10]{0:T(128)S(1)}, f32[10]{0:T(128)}, u32[]{:S(2)}) copy-start(f32[10]{0:T(128)} %equil.1) | copy-start | bytes 124

commit v2 on v1

v2 whole, which is shorter than its diff:
```python
import functools

import jax
import jax.numpy as jnp
from jax import lax
from jax.experimental import pallas as pl
from jax.experimental.pallas import tpu as pltpu
from jax.sharding import PartitionSpec as P

MESH = pl.DeviceIdType.MESH
loop = lax.fori_loop
NF = 64
DT = 0.2
FL = 8
NS = 10
ROWS = 16
CELLS = 1024
QUARTER = 256
CHUNK = 128
HALF = NS // 2


def kernel(
    n_az,
    q_in, w_in, vel_in, dif_in, mix_in, rate_in, equil_in,
    adv_out, den_out,
    q, u, w, gas, gas_own, h1, h2, eh, sums, got, got_x, total, corr, corr_got, e1, e2, heat, heat_got, rate, equil,
    load_sem, gas_s, gas_r, h1_s, h1_r, h2_s, h2_r, eh_s, eh_r, red_s, red_r, cor_s, cor_r, den_s, den_r,
):
    f = lax.axis_index("field")
    a = lax.axis_index("azim")
    y, xl = f // 2, f % 2
    yp, yo, ym = (y + 1) % 4, (y + 2) % 4, (y + 3) % 4
    dev_p, dev_m, dev_o, dev_x = (yp * 2 + xl, a), (ym * 2 + xl, a), (yo * 2 + xl, a), (y * 2 + 1 - xl, a)
    around = ((yo, dev_o), (yp, dev_p), (ym, dev_m))
    dev_up, dev_dn = (f, (a + 1) % n_az), (f, (a + n_az - 1) % n_az)

    def peer(k):
        return (f + k) % 8

    def chunk(i):
        return pl.ds(pl.multiple_of(i * CHUNK, CHUNK), CHUNK)

    def quarter(i):
        return pl.ds(pl.multiple_of(i * QUARTER, QUARTER), QUARTER)

    def remote(src, dst, send, recv, device):
        return pltpu.make_async_remote_copy(
            src_ref=src, dst_ref=dst, send_sem=send, recv_sem=recv,
            device_id=device, device_id_type=MESH,
        )

    def start(copies):
        for c in copies:
            c.start()

    def arrive(copies):
        for c in copies:
            c.wait_recv()

    loads = [pltpu.make_async_copy(q_in.at[i], q.at[i], load_sem.at[i]) for i in range(FL)]
    gas_loads = [
        pltpu.make_async_copy(r, gas_own.at[i], load_sem.at[FL + 1 + i])
        for i, r in enumerate((vel_in, dif_in, mix_in))
    ]
    other_loads = [
        pltpu.make_async_copy(w_in, w, load_sem.at[FL]),
        pltpu.make_async_copy(rate_in, rate, load_sem.at[FL + 4]),
        pltpu.make_async_copy(equil_in, equil, load_sem.at[FL + 5]),
    ]

    barrier = pltpu.get_barrier_semaphore()
    first_slab = 1 - jnp.minimum(a, 1)

    def greet(device):
        pl.semaphore_signal(barrier, inc=1, device_id=device, device_id_type=MESH)

    for k in range(1, 8):
        greet((peer(k), a))
    pl.when(a != n_az - 1)(lambda: greet(dev_up))
    pl.when(a != 0)(lambda: greet(dev_dn))
    for c in gas_loads + loads + other_loads:
        c.start()
    pl.semaphore_wait(barrier, 9 - first_slab)
    pl.when(a == 0)(lambda: greet(dev_dn))
    pl.when(a == n_az - 1)(lambda: greet(dev_up))

    for c in gas_loads:
        c.wait()
    gas_sends = [
        remote(gas_own, gas.at[:, :, chunk(f)], gas_s.at[k], gas_r.at[k], (peer(k + 1), a))
        for k in range(7)
    ]
    start(gas_sends)
    gas[:, :, chunk(f)] = gas_own[...]

    halo1 = [
        remote(q_in.at[:, :, pl.ds(ROWS - 1, 1), :], h1.at[0], h1_s.at[0], h1_r.at[0], dev_up),
        remote(q_in.at[:, :, pl.ds(0, 1), :], h1.at[1], h1_s.at[1], h1_r.at[1], dev_dn),
    ]
    halo1[0].start()
    pl.when(a != 0)(lambda: halo1[1].start())

    def late_halo():
        def send():
            pl.semaphore_wait(barrier, 1)
            halo1[1].start()

        pl.when(a == 0)(send)

    def part(p):
        return pl.ds(p * HALF, HALF)

    def red(n, p, i, src, dst, device):
        return remote(src, dst, red_s.at[n * 2 + p, i], red_r.at[n * 2 + p, i], device)

    def scatter(n, p, i):
        k, device = around[i]
        return red(n, p, i, sums.at[n, part(p), :, quarter(k)], got.at[n, p, i], device)

    def exchange(n, p):
        return red(n, p, 3, sums.at[n, part(p), :, quarter(y)], got_x.at[n, p], dev_x)

    def gather(n, p, i):
        piece = total.at[n, part(p), :, quarter(y)]
        return red(n, p, 4 + i, piece, piece, around[i][1])

    def after_scatter(n, p):
        arrive([scatter(n, p, i) for i in range(3)])

        def add(i, _):
            cols = quarter(y)
            sums[n, p * HALF + i, :, cols] += got[n, p, 0, i] + (got[n, p, 1, i] + got[n, p, 2, i])
            return 0

        loop(0, HALF, add, 0)
        exchange(n, p).start()

    def after_exchange(n, p):
        exchange(n, p).wait_recv()

        def add(i, _):
            for j in range(2):
                cols, part_cols = chunk(2 * y + j), pl.ds(j * CHUNK, CHUNK)
                for t in range(2):
                    v = sums[n, p * HALF + i, tiles[t], cols] + got_x[n, p, i, tiles[t], part_cols]
                    if n == 1:
                        edge = corr[t, p * HALF + i, :, cols]
                        for k in range(7):
                            edge = edge + corr_got[k, t, p * HALF + i, :, part_cols]
                        v = v + jnp.where((first, last)[t], jnp.broadcast_to(edge, (8, CHUNK)), 0.0)
                    total[n, p * HALF + i, tiles[t], cols] = v
            return 0

        loop(0, HALF, add, 0)
        start([gather(n, p, i) for i in range(3)])

    row = lax.broadcasted_iota(jnp.int32, (8, CHUNK), 0)
    first, last = row == 0, row == 7
    tiles = (pl.ds(0, 8), pl.ds(8, 8))

    def sum_q(k):
        def body(s, _):
            acc = q[0, s, :, quarter(k)]
            for i in range(1, FL):
                acc = acc + q[i, s, :, quarter(k)]
            sums[0, s, :, quarter(k)] = acc
            return 0

        loop(0, NS, body, 0)

    for c in loads:
        c.wait()
    for i, (k, _) in enumerate(around):
        sum_q(k)
        start([scatter(0, p, i) for p in range(2)])
    sum_q(y)

    def neighbours(lower, upper, below, above):
        lower_up, upper_up = pltpu.roll(lower, 7, 0), pltpu.roll(upper, 7, 0)
        lower_dn, upper_dn = pltpu.roll(lower, 1, 0), pltpu.roll(upper, 1, 0)
        up = (jnp.where(last, upper_up, lower_up), jnp.where(last, above, upper_up))
        dn = (jnp.where(first, below, lower_dn), jnp.where(first, lower_dn, upper_dn))
        return up, dn

    def coefficients(cols, t):
        vel, dif, mix = gas[0, tiles[t], cols], gas[1, tiles[t], cols], gas[2, tiles[t], cols]
        keep = 1.0 - (2.0 * DT) * dif - (0.5 * DT) * mix
        return keep, DT * dif, (-0.5 * DT) * vel, 0.5 * jnp.sqrt(2.0 * dif)

    def burn(x):
        heating = 1.0 + 0.5 * x * x
        return DT * jnp.exp(1.0 - 1.0 / heating)

    zero = jnp.zeros((8, CHUNK), jnp.float32)

    def explicit(k):
        def column(j, _):
            cols = chunk(k * 2 + j)
            co = [coefficients(cols, t) for t in range(2)]

            def field(i, acc):
                grad_c = [co[t][2] + co[t][3] * w[i, tiles[t], cols] for t in range(2)]
                b = [burn(q[i, 0, tiles[t], cols]) for t in range(2)]
                out = []
                for s in range(NS):
                    x = [q[i, s, tiles[t], cols] for t in range(2)]
                    up, dn = neighbours(x[0], x[1], zero, zero)
                    for t in range(2):
                        v = (
                            x[t] * co[t][0]
                            + (up[t] - dn[t]) * grad_c[t]
                            + (up[t] + dn[t]) * co[t][1]
                            + (rate[s] * b[t]) * (equil[s] - x[t])
                        )
                        u[i, s, tiles[t], cols] = v
                        out.append(acc[2 * s + t] + v)
                return tuple(out)

            acc = loop(0, FL, field, (zero,) * (2 * NS))
            for s in range(NS):
                for t in range(2):
                    sums[1, s, tiles[t], cols] = acc[2 * s + t]
            return 0

        loop(0, 2, column, 0)

    def edges():
        def column(j, _):
            cols = chunk(j)
            co = [coefficients(cols, t) for t in range(2)]

            def field(i, acc):
                grad_c = [co[t][2] + co[t][3] * w[i, tiles[t], cols] for t in range(2)]
                coef = (jnp.where(first, co[0][1] - grad_c[0], 0.0), jnp.where(last, co[1][1] + grad_c[1], 0.0))
                out = []
                for s in range(NS):
                    for t in range(2):
                        v = jnp.broadcast_to(h1[t, i, s, :, cols], (8, CHUNK)) * coef[t]
                        u[i, s, tiles[t], cols] += v
                        out.append(acc[2 * s + t] + v)
                return tuple(out)

            acc = loop(0, FL, field, (zero,) * (2 * NS))
            for s in range(NS):
                corr[0, s, :, cols] = acc[2 * s][0:1]
                corr[1, s, :, cols] = acc[2 * s + 1][7:8]
            return 0

        loop(0, CELLS // CHUNK, column, 0)

    def corrections():
        out = []
        for k in range(7):
            owner = peer(k + 1)
            piece = corr.at[:, :, :, quarter(owner // 2)]
            out.append(remote(piece, corr_got.at[k], cor_s.at[k], cor_r.at[k], (owner, a)))
        return out

    halo2 = [
        remote(u.at[:, :, pl.ds(ROWS - 1, 1), :], h2.at[0], h2_s.at[0], h2_r.at[0], dev_up),
        remote(u.at[:, :, pl.ds(0, 1), :], h2.at[1], h2_s.at[1], h2_r.at[1], dev_dn),
    ]

    def mean_rows(p):
        return [
            remote(e1.at[part(p), pl.ds(ROWS - 1, 1), :], eh.at[0, part(p)], eh_s.at[0, p], eh_r.at[0, p], dev_up),
            remote(e1.at[part(p), pl.ds(0, 1), :], eh.at[1, part(p)], eh_s.at[1, p], eh_r.at[1, p], dev_dn),
        ]

    def mixing(p):
        arrive([gather(0, p, i) for i in range(3)])

        def body(i, _):
            e1[p * HALF + i] = (0.5 * DT / NF) * gas[2] * total[0, p * HALF + i]
            return 0

        loop(0, HALF, body, 0)
        start(mean_rows(p))

    def second(k, scalars):
        def column(j, _):
            cols = chunk(k * 2 + j)
            half = [tuple(0.5 * c for c in coefficients(cols, t)) for t in range(2)]
            for s in scalars:
                for t in range(2):
                    m = (0.25 * DT) * gas[2, tiles[t], cols]
                    e2[s, tiles[t], :] = m * ((1.0 / NF) * total[1, s, tiles[t], cols] + e1[s, tiles[t], cols])

            def field(i, acc):
                grad_c = [half[t][2] + half[t][3] * w[i, tiles[t], cols] for t in range(2)]
                b = [0.5 * burn(u[i, 0, tiles[t], cols] + e1[0, tiles[t], cols]) for t in range(2)]
                out = list(acc)
                for s in scalars:
                    x = [u[i, s, tiles[t], cols] + e1[s, tiles[t], cols] for t in range(2)]
                    below = jnp.broadcast_to(h2[0, i, s, :, cols] + eh[0, s, :, cols], (8, CHUNK))
                    above = jnp.broadcast_to(h2[1, i, s, :, cols] + eh[1, s, :, cols], (8, CHUNK))
                    up, dn = neighbours(x[0], x[1], below, above)
                    for t in range(2):
                        v = (
                            0.5 * q[i, s, tiles[t], cols]
                            + x[t] * half[t][0]
                            + (up[t] - dn[t]) * grad_c[t]
                            + (up[t] + dn[t]) * half[t][1]
                            + e2[s, tiles[t], :]
                            + (rate[s] * b[t]) * (equil[s] - x[t])
                        )
                        adv_out[i, s, tiles[t], cols] = v
                        if s == 0:
                            out[t] = out[t] + (1.0 + 0.5 * v * v)
                return tuple(out)

            acc = loop(0, FL, field, (zero,) * 2)
            if 0 in scalars:
                for t in range(2):
                    heat[tiles[t], cols] = acc[t]
            return 0

        loop(0, 2, column, 0)

    def den(k, n):
        out = []
        for side in range(2 if n else 1):
            owner = k * 2 + ((xl + side) % 2 if n else 1 - xl)
            out.append(
                remote(heat.at[:, chunk(owner)], heat_got.at[n, side], den_s.at[n, side], den_r.at[n, side], (owner, a))
            )
        return out

    arrive(gas_sends)
    for c in other_loads:
        c.wait()
    for i, (k, _) in enumerate(around):
        explicit(k)
        start([scatter(1, p, i) for p in range(2)])
    after_scatter(0, 0)
    after_scatter(0, 1)
    explicit(y)
    late_halo()
    after_exchange(0, 0)
    after_exchange(0, 1)
    arrive(halo1)
    edges()
    start(corrections())
    start(halo2)
    after_scatter(1, 0)
    after_scatter(1, 1)
    arrive(corrections())
    after_exchange(1, 0)
    after_exchange(1, 1)
    mixing(0)
    mixing(1)
    arrive(halo2)
    for p in range(2):
        scalars = tuple(range(p * HALF, p * HALF + HALF))
        arrive(mean_rows(p))
        for n, (k, i) in enumerate(((y, None), (yp, 2), (ym, 1), (yo, 0))):
            if n:
                gather(1, p, i).wait_recv()
            second(k, scalars)
            if p == 0:
                start(den(k, n))

    heat_sum = heat[:, chunk(f)]
    for n, k in enumerate((y, yp, ym, yo)):
        for i, c in enumerate(den(k, n)):
            c.wait_recv()
            heat_sum = heat_sum + heat_got[n, i]
    den_out[...] = 1.0 / (heat_sum * (1.0 / NF))

    for n, k in enumerate((y, yp, ym, yo)):
        for c in den(k, n):
            c.wait_send()
    for c in gas_sends + halo1 + halo2 + mean_rows(0) + mean_rows(1) + corrections():
        c.wait_send()
    for n in range(2):
        for p in range(2):
            for c in [scatter(n, p, i) for i in range(3)] + [exchange(n, p)] + [gather(n, p, i) for i in range(3)]:
                c.wait_send()


def solution(mesh):
    n_az = mesh.shape["azim"]

    def shards(scalars, wiener, velocity, diffusivity, mix_rate, reaction_rate, equilibrium):
        hbm = pl.BlockSpec(memory_space=pltpu.HBM)
        vmem = pl.BlockSpec(memory_space=pltpu.VMEM)
        f32 = jnp.float32
        dma = pltpu.SemaphoreType.DMA
        return pl.pallas_call(
            functools.partial(kernel, n_az),
            out_shape=(
                jax.ShapeDtypeStruct((FL, NS, ROWS, CELLS), f32),
                jax.ShapeDtypeStruct((ROWS, CHUNK), f32),
            ),
            in_specs=[hbm] * 7,
            out_specs=(vmem, vmem),
            scratch_shapes=[
                pltpu.VMEM((FL, NS, ROWS, CELLS), f32),
                pltpu.VMEM((FL, NS, ROWS, CELLS), f32),
                pltpu.VMEM((FL, ROWS, CELLS), f32),
                pltpu.VMEM((3, ROWS, CELLS), f32),
                pltpu.VMEM((3, ROWS, CHUNK), f32),
                pltpu.VMEM((2, FL, NS, 1, CELLS), f32),
                pltpu.VMEM((2, FL, NS, 1, CELLS), f32),
                pltpu.VMEM((2, NS, 1, CELLS), f32),
                pltpu.VMEM((2, NS, ROWS, CELLS), f32),
                pltpu.VMEM((2, 2, 3, HALF, ROWS, QUARTER), f32),
                pltpu.VMEM((2, 2, HALF, ROWS, QUARTER), f32),
                pltpu.VMEM((2, NS, ROWS, CELLS), f32),
                pltpu.VMEM((2, NS, 1, CELLS), f32),
                pltpu.VMEM((7, 2, NS, 1, QUARTER), f32),
                pltpu.VMEM((NS, ROWS, CELLS), f32),
                pltpu.VMEM((NS, ROWS, CHUNK), f32),
                pltpu.VMEM((ROWS, CELLS), f32),
                pltpu.VMEM((4, 2, ROWS, CHUNK), f32),
                pltpu.SMEM((NS,), f32),
                pltpu.SMEM((NS,), f32),
                dma((FL + 6,)),
                dma((7,)), dma((7,)),
                dma((2,)), dma((2,)),
                dma((2,)), dma((2,)),
                dma((2, 2)), dma((2, 2)),
                dma((4, 7)), dma((4, 7)),
                dma((7,)), dma((7,)),
                dma((4, 2)), dma((4, 2)),
            ],
            compiler_params=pltpu.CompilerParams(
                collective_id=0, has_side_effects=True, vmem_limit_bytes=48 << 20
            ),
            name="fields_step",
        )(
            *(
                pltpu.with_memory_space_constraint(x, pltpu.HBM)
                for x in (scalars, wiener, velocity, diffusivity, mix_rate, reaction_rate, equilibrium)
            )
        )

    return jax.shard_map(
        shards,
        mesh=mesh,
        in_specs=(
            P("field", None, "azim", None),
            P("field", "azim", None),
            P("azim", "field"),
            P("azim", "field"),
            P("azim", "field"),
            P(),
            P(),
        ),
        out_specs=(P("field", None, "azim", None), P("azim", "field")),
        check_vma=False,
    )
```

time: 62.9 us -> 53.7 us (0.85)
  Pallas kernels: 54 us -> 49.5 us
  local copies, waits for them, and re-layouts: 7.39 us -> 2.96 us
    pallas_call x1, Pallas kernels: 54 us -> 49.5 us  [shards(): pl.pallas_call(functools.partial(kernel, n_az), out_shape=(jax.ShapeDtype...]
    unnamed x14 -> x2, local copies, waits for them, and re-layouts: 7.39 us -> 2.96 us
where the time goes in v2:
time: 53.7 us; the launch traced here: 53.1 us
  Pallas kernels  49.5 us (92%)
  local copies, waits for them, and re-layouts  2.96 us (6%)
  between operations  0.64 us (1%)
    pallas_call x1, Pallas kernels, shards(): pl.pallas_call(functools.partial(kernel, n_az), out_shape=(jax.ShapeDtype...  49.5 us
    unnamed x2, local copies, waits for them, and re-layouts  2.96 us

profile of v2, /device:TPU:2, one launch (start us, length us, event | category | flops | bytes accessed | tf_op | source)
XLA Modules:
  0.0 53.1 jit_solution(17425973377241583897)
XLA Ops:
  0.6 49.5 %fields_step.1 = (f32[8,10,16,1024]{3,2,1,0:T(8,128)S(1)}, f32[16,128]{1,0:T(8,128)S(1)}) custom-call(f32[8,10,16,1024]{3,2,1,0:T(8,128)} %q_in.1, f32[8,16,1024]{2,1,0:T(8,128)} %w_in.1, f32[16,128]{1,0:T(8,128)} %vel_in.1, f32[16,128]{1,0:T(8,128)} %dif_in.1, f32[16,128]{1,0:T(8,128)} %mix_in.1, f32[10]{0:T(128)} %rate_in.1, f32[10]{0:T(128)} %equil_in.1), custom_call_target="tpu_custom_call" | custom-call | tf_op jit(solution)/shard_map/fields_step/pallas_call | solution.py:390
  50.1 2.4 %copy.11 = f32[8,10,16,1024]{3,2,1,0:T(8,128)} copy(f32[8,10,16,1024]{3,2,1,0:T(8,128)S(1)} %get-tuple-element.4) | data formatting | bytes 10485760
  52.5 0.6 %copy.12 = f32[16,128]{1,0:T(8,128)} copy(f32[16,128]{1,0:T(8,128)S(1)} %get-tuple-element.5) | data formatting | bytes 16384

commit v3 on v2

--- a/solution.py
+++ b/solution.py
@@ -337,19 +337,19 @@
     after_scatter(0, 1)
     explicit(y)
     late_halo()
-    after_exchange(0, 0)
-    after_exchange(0, 1)
     arrive(halo1)
     edges()
     start(corrections())
-    start(halo2)
     after_scatter(1, 0)
     after_scatter(1, 1)
+    start(halo2)
+    after_exchange(0, 0)
+    after_exchange(0, 1)
+    mixing(0)
+    mixing(1)
     arrive(corrections())
     after_exchange(1, 0)
     after_exchange(1, 1)
-    mixing(0)
-    mixing(1)
     arrive(halo2)
     for p in range(2):
         scalars = tuple(range(p * HALF, p * HALF + HALF))

time: 53.7 us -> 51.5 us (0.959)
  Pallas kernels: 49.5 us -> 47.1 us
    pallas_call x1, Pallas kernels: 49.5 us -> 47.1 us  [shards(): pl.pallas_call(functools.partial(kernel, n_az), out_shape=(jax.ShapeDtype...]
where the time goes in v3:
time: 51.5 us; the launch traced here: 50.7 us
  Pallas kernels  47.1 us (91%)
  local copies, waits for them, and re-layouts  2.96 us (6%)
  between operations  0.64 us (1%)
    pallas_call x1, Pallas kernels, shards(): pl.pallas_call(functools.partial(kernel, n_az), out_shape=(jax.ShapeDtype...  47.1 us
    unnamed x2, local copies, waits for them, and re-layouts  2.96 us

profile of v3, /device:TPU:2, one launch (start us, length us, event | category | flops | bytes accessed | tf_op | source)
XLA Modules:
  0.0 50.7 jit_solution(10591650617952462547)
XLA Ops:
  0.6 47.1 %fields_step.1 = (f32[8,10,16,1024]{3,2,1,0:T(8,128)S(1)}, f32[16,128]{1,0:T(8,128)S(1)}) custom-call(f32[8,10,16,1024]{3,2,1,0:T(8,128)} %q_in.1, f32[8,16,1024]{2,1,0:T(8,128)} %w_in.1, f32[16,128]{1,0:T(8,128)} %vel_in.1, f32[16,128]{1,0:T(8,128)} %dif_in.1, f32[16,128]{1,0:T(8,128)} %mix_in.1, f32[10]{0:T(128)} %rate_in.1, f32[10]{0:T(128)} %equil_in.1), custom_call_target="tpu_custom_call" | custom-call | tf_op jit(solution)/shard_map/fields_step/pallas_call | solution.py:390
  47.8 2.4 %copy.11 = f32[8,10,16,1024]{3,2,1,0:T(8,128)} copy(f32[8,10,16,1024]{3,2,1,0:T(8,128)S(1)} %get-tuple-element.4) | data formatting | bytes 10485760
  50.1 0.6 %copy.12 = f32[16,128]{1,0:T(8,128)} copy(f32[16,128]{1,0:T(8,128)S(1)} %get-tuple-element.5) | data formatting | bytes 16384

commit v4 on v3

--- a/solution.py
+++ b/solution.py
@@ -351,15 +351,18 @@
     after_exchange(1, 0)
     after_exchange(1, 1)
     arrive(halo2)
+    parts = [tuple(range(p * HALF, p * HALF + HALF)) for p in range(2)]
+    arrive(mean_rows(0))
+    second(y, parts[0])
+    start(den(y, 0))
+    arrive(mean_rows(1))
+    second(y, parts[1])
     for p in range(2):
-        scalars = tuple(range(p * HALF, p * HALF + HALF))
-        arrive(mean_rows(p))
-        for n, (k, i) in enumerate(((y, None), (yp, 2), (ym, 1), (yo, 0))):
-            if n:
-                gather(1, p, i).wait_recv()
-            second(k, scalars)
+        for n, (k, i) in enumerate(((yp, 2), (ym, 1), (yo, 0))):
+            gather(1, p, i).wait_recv()
+            second(k, parts[p])
             if p == 0:
-                start(den(k, n))
+                start(den(k, n + 1))
 
     heat_sum = heat[:, chunk(f)]
     for n, k in enumerate((y, yp, ym, yo)):

time: 51.5 us -> 52.6 us (1.021); the launches traced: 50.7 us -> 52.5 us
  Pallas kernels: 47.1 us -> 48.9 us
    pallas_call x1, Pallas kernels: 47.1 us -> 48.9 us  [shards(): pl.pallas_call(functools.partial(kernel, n_az), out_shape=(jax.ShapeDtype...]
where the time goes in v4:
time: 52.6 us; the launch traced here: 52.5 us
  Pallas kernels  48.9 us (93%)
  local copies, waits for them, and re-layouts  2.96 us (6%)
  between operations  0.64 us (1%)
    pallas_call x1, Pallas kernels, shards(): pl.pallas_call(functools.partial(kernel, n_az), out_shape=(jax.ShapeDtype...  48.9 us
    unnamed x2, local copies, waits for them, and re-layouts  2.96 us

profile of v4, /device:TPU:2, one launch (start us, length us, event | category | flops | bytes accessed | tf_op | source)
XLA Modules:
  0.0 52.5 jit_solution(1065095763807162906)
XLA Ops:
  0.6 48.9 %fields_step.1 = (f32[8,10,16,1024]{3,2,1,0:T(8,128)S(1)}, f32[16,128]{1,0:T(8,128)S(1)}) custom-call(f32[8,10,16,1024]{3,2,1,0:T(8,128)} %q_in.1, f32[8,16,1024]{2,1,0:T(8,128)} %w_in.1, f32[16,128]{1,0:T(8,128)} %vel_in.1, f32[16,128]{1,0:T(8,128)} %dif_in.1, f32[16,128]{1,0:T(8,128)} %mix_in.1, f32[10]{0:T(128)} %rate_in.1, f32[10]{0:T(128)} %equil_in.1), custom_call_target="tpu_custom_call" | custom-call | tf_op jit(solution)/shard_map/fields_step/pallas_call | solution.py:393
  49.6 2.4 %copy.11 = f32[8,10,16,1024]{3,2,1,0:T(8,128)} copy(f32[8,10,16,1024]{3,2,1,0:T(8,128)S(1)} %get-tuple-element.4) | data formatting | bytes 10485760
  51.9 0.6 %copy.12 = f32[16,128]{1,0:T(8,128)} copy(f32[16,128]{1,0:T(8,128)S(1)} %get-tuple-element.5) | data formatting | bytes 16384
